TPU v7x, 256 devices: a whole 4x4x8 slice. The times are simulated.
256 devices in a mesh: grp: 16 (over z, core), ep: 16 (over y, x).
Axes of the slice: x: 4, y: 4, z: 8, core: 2. Of those that a mesh axis runs over, the one named last changes fastest.
Arguments:
- queries: bfloat16 [1024, 64, 576], P(('grp', 'ep')), may hold values from -75 to 75
- cache: bfloat16 [1024, 256, 576], P(('grp', 'ep')), may hold values from -6 to 6
- lengths: int32 [1024], P(('grp', 'ep')), may hold values from 2 to 256, as said below
- live_rows: int32 [256], P(('grp', 'ep')), may hold values from 1 to 4, as said below
- tokens: bfloat16 [4096, 3584], P(('grp', 'ep')), may hold values from -6 to 6
- ids: int32 [4096, 8], P(('grp', 'ep')), may hold values from 0 to 127, all different within a row; in each aligned block of 16 rows (0 to 15, 16 to 31, ...) at most 2 rows name the same one
- gates: float32 [4096, 8], P(('grp', 'ep')), may hold values from 0.1 to 1
- w_gate: bfloat16 [256, 3584, 512], P(('grp', 'ep')), may hold values from -0.09375 to 0.09375
- w_up: bfloat16 [256, 3584, 512], P(('grp', 'ep')), may hold values from -0.09375 to 0.09375
- w_down: bfloat16 [256, 512, 3584], P(('grp', 'ep')), may hold values from -0.1875 to 0.1875
Outputs:
- context: bfloat16 [1024, 64, 512], P(('grp', 'ep'))
- mixed: bfloat16 [4096, 3584], P(('grp', 'ep'))
Inputs may be any that keep to these rules, and one draw needn't show every extreme that they name: `ids`: each row names 8 different experts; among the rows of one device no expert is named more than 2 times. `lengths`: the first request slot of every device holds 256 positions. `live_rows`: a device's live request slots are its first ones; on a quarter of the grp indices every device holds 2 or fewer, elsewhere exactly 4.
All inputs are finite; a program needn't handle non-finite values.
Results may differ from a plain program's by a relative error of at most 0.012.
Values may be sent and summed in bfloat16 or wider, within the bound.
A program may use at most 128 MiB of HBM per device.

v0:
```python
import jax
import jax.numpy as jnp
from jax import lax
from jax.sharding import PartitionSpec as P

TOPK = 8
LAT = 512
CAP = 2
score_scale = 192.0 ** (-0.5)
neg_large = -1e30


def attend(queries, cache, lengths, live_count):
    scores = (
        jnp.einsum("rhc,rlc->rhl", queries, cache, preferred_element_type=jnp.float32) * score_scale
    )
    positions = lax.broadcasted_iota(jnp.int32, scores.shape, 2)
    inside = positions < lengths[:, None, None]
    masked = jnp.where(inside, scores, neg_large)
    highest = jnp.max(masked, axis=2, keepdims=True)
    powers = jnp.where(inside, jnp.exp(masked - highest), 0.0)
    totals = jnp.sum(powers, axis=2, keepdims=True)
    weights = (powers / totals).astype(jnp.bfloat16)
    context = jnp.einsum(
        "rhl,rlc->rhc", weights, cache[:, :, :LAT], preferred_element_type=jnp.float32
    ).astype(jnp.bfloat16)
    request_slot = lax.broadcasted_iota(jnp.int32, context.shape, 0)
    return jnp.where(request_slot < live_count, context, jnp.zeros_like(context))


def expert_partial(flat_rows, w_gate, w_up, w_down):
    gate_part = jnp.dot(flat_rows, w_gate[0], preferred_element_type=jnp.float32)
    up_part = jnp.dot(flat_rows, w_up[0], preferred_element_type=jnp.float32)
    hidden = (jax.nn.silu(gate_part) * up_part).astype(jnp.bfloat16)
    return jnp.dot(hidden, w_down[0], preferred_element_type=jnp.float32)


def per_device(queries, cache, lengths, live_rows, tokens, ids, gates, w_gate, w_up, w_down):
    context = attend(queries, cache, lengths, live_rows[0])
    group_count = lax.axis_size("grp")
    peer_count = lax.axis_size("ep")
    pair_count = peer_count // 2
    row_count = tokens.shape[0]
    feature = tokens.shape[1]
    expert_slots = group_count * CAP
    slot_count = pair_count * expert_slots
    column_rows = group_count * row_count
    gate_high = gates.astype(jnp.bfloat16)
    gate_low = (gates - gate_high.astype(jnp.float32)).astype(jnp.bfloat16)
    meta = jnp.concatenate([ids.astype(jnp.bfloat16), gate_high, gate_low], axis=1)
    meta = jnp.pad(meta, ((0, 0), (0, 128 - meta.shape[1])))
    packed = lax.all_gather(jnp.concatenate([tokens, meta], axis=1), "grp", axis=0, tiled=True)
    all_tokens = packed[:, :feature]
    all_ids = packed[:, feature : feature + TOPK].astype(jnp.int32)
    all_gates = packed[:, feature + TOPK : feature + 2 * TOPK].astype(jnp.float32) + packed[
        :, feature + 2 * TOPK : feature + 3 * TOPK
    ].astype(jnp.float32)
    my_group = lax.axis_index("grp")
    local = all_ids - pair_count * my_group
    experts = jnp.arange(pair_count, dtype=jnp.int32)
    pick_hot = (local[:, :, None] == experts[None, None, :]).astype(jnp.int32)
    token_hot = jnp.sum(pick_hot, axis=1)
    gate_of = jnp.sum(all_gates[:, :, None] * pick_hot.astype(jnp.float32), axis=1)
    blocks = token_hot.reshape(group_count, row_count, pair_count)
    earlier = (jnp.cumsum(blocks, axis=1) - blocks).reshape(column_rows, pair_count)
    source = jnp.arange(column_rows, dtype=jnp.int32)[:, None] // row_count
    slot_id = experts[None, :] * expert_slots + source * CAP + earlier
    slot_id = jnp.where(token_hot > 0, slot_id, slot_count)
    slots = jnp.arange(slot_count, dtype=jnp.int32)
    match = slot_id[:, :, None] == slots[None, None, :]
    dispatch = jnp.any(match, axis=1).T.astype(jnp.bfloat16)
    combine = jnp.sum(jnp.where(match, gate_of[:, :, None], 0.0), axis=1)
    outgoing = jnp.dot(dispatch, all_tokens, preferred_element_type=jnp.float32).astype(
        jnp.bfloat16
    )
    doubled = jnp.repeat(outgoing.reshape(pair_count, expert_slots, feature), 2, axis=0)
    arriving = lax.all_to_all(doubled, "ep", split_axis=0, concat_axis=0, tiled=True)
    partials = expert_partial(
        arriving.reshape(peer_count * expert_slots, feature), w_gate, w_up, w_down
    ).astype(jnp.bfloat16)
    returned = lax.all_to_all(
        partials.reshape(peer_count, expert_slots, feature),
        "ep",
        split_axis=0,
        concat_axis=0,
        tiled=True,
    )
    expert_out = (
        returned.reshape(pair_count, 2, expert_slots, feature)
        .astype(jnp.float32)
        .sum(axis=1)
        .astype(jnp.bfloat16)
        .reshape(slot_count, feature)
    )
    column_mixed = jnp.dot(
        combine,
        expert_out.astype(jnp.float32),
        precision=lax.Precision.HIGHEST,
        preferred_element_type=jnp.float32,
    )
    mixed = lax.psum_scatter(
        column_mixed.astype(jnp.bfloat16), "grp", scatter_dimension=0, tiled=True
    )
    return (context, mixed)


def solution(mesh):
    in_specs = (
        P(("grp", "ep"), None, None),
        P(("grp", "ep"), None, None),
        P(("grp", "ep")),
        P(("grp", "ep")),
        P(("grp", "ep"), None),
        P(("grp", "ep"), None),
        P(("grp", "ep"), None),
        P(("grp", "ep"), None, None),
        P(("grp", "ep"), None, None),
        P(("grp", "ep"), None, None),
    )
    out_specs = (P(("grp", "ep"), None, None), P(("grp", "ep"), None))
    return jax.shard_map(
        per_device, mesh=mesh, in_specs=in_specs, out_specs=out_specs, check_vma=False
    )
```

profile of v0, /device:TPU:6, one launch (start us, length us, event | category | flops | bytes accessed | tf_op | source)
XLA Modules:
  0.0 250.5 jit_solution(11067031756763123263)
XLA Ops:
  7.2 0.0 copy-start
  7.2 0.0 all-gather.2.cloned.1.call-start
  7.2 0.8 copy.35
  8.0 0.8 copy.34
  8.8 0.1 fusion.30
  8.9 1.6 pad_maximum_fusion
  10.4 0.0 all-gather.2.cloned.1.call-update
  10.5 42.6 %all-gather.2.cloned.1.call-done = bf16[256,3712]{1,0:T(8,128)(2,1)} async-done(((bf16[16,3712]{1,0:T(8,128)(2,1)}), bf16[256,3712]{1,0:T(8,128)(2,1)}) %all-gather.2.cloned.1.call-update) | async-done | bytes 1900560 | tf_op jit(solution)/shard_map/all_gather | solution.py:52
  53.1 1.1 fusion.35
  54.2 0.1 copy.45
  54.3 0.1 reshape.114
  54.4 0.1 copy.38
  54.5 0.7 fusion.37
  55.2 0.1 copy.39
  55.3 0.1 reduce_window_sum.14
  55.4 0.1 add_select_fusion
  55.5 0.1 copy.40
  55.6 0.7 fusion.6
  56.3 2.2 convolution_convert_fusion.2
  58.5 0.4 broadcast_in_dim.46
  58.9 0.0 copy-start.4
  58.9 50.4 %all_to_all.10 = bf16[16,32,3584]{2,1,0:T(8,128)(2,1)S(1)} all-to-all(bf16[16,32,3584]{2,1,0:T(8,128)(2,1)S(1)} %bitcast.38), channel_id=1, replica_groups=mesh['grp'=16,'ep'=16] {'ep'}, dimensions={0} | all-to-all | bytes 7340032 | tf_op jit(solution)/shard_map/all_to_all | solution.py:77
  109.3 0.0 copy-start.1
  109.3 1.8 copy-done.1
  111.1 0.0 copy-done.4
  111.1 2.0 fusion.4
  113.2 10.0 %convolution_convert_fusion = bf16[512,3584]{1,0:T(8,128)(2,1)} fusion(bf16[1,512,3584]{2,1,0:T(8,128)(2,1)} %param.19, bf16[512,3584]{1,0:T(8,128)(2,1)} %bitcast.43, bf16[1,3584,512]{2,1,0:T(8,128)(2,1)} %param.18, f32[512,512]{1,0:T(8,128)S(1)} %fusion.4), kind=kOutput, calls=%fused_computation.1 | convolution fusion | flops 3761504256 | bytes 15728640 | tf_op jit(solution)/shard_map/dot_general | solution.py:35
  123.2 7.0 %all-to-all-start.1 = ((bf16[16,32,3584]{2,1,0:T(8,128)(2,1)}), bf16[16,32,3584]{2,1,0:T(8,128)(2,1)}, u32[]{:S(2)}, u32[]{:S(2)}) async-start(bf16[16,32,3584]{2,1,0:T(8,128)(2,1)} %bitcast.41), calls=%async_computation.1 | async-start | bytes 7340032 | tf_op jit(solution)/shard_map/all_to_all | solution.py:81
  130.2 0.0 reduce-scatter.2.cloned.1.call-start
  130.3 0.1 copy.46
  130.3 0.1 copy.47
  130.5 0.1 copy.43
  130.6 1.5 select_reduce_fusion
  132.1 48.8 %all-to-all-done.1 = bf16[16,32,3584]{2,1,0:T(8,128)(2,1)} async-done(((bf16[16,32,3584]{2,1,0:T(8,128)(2,1)}), bf16[16,32,3584]{2,1,0:T(8,128)(2,1)}, u32[]{:S(2)}, u32[]{:S(2)}) %all-to-all-start.1) | async-done | bytes 3670048 | tf_op jit(solution)/shard_map/all_to_all | solution.py:81
  180.9 2.8 %bitcast_reduce_fusion = bf16[8,32,3584]{2,1,0:T(8,128)(2,1)S(1)} fusion(bf16[16,32,3584]{2,1,0:T(8,128)(2,1)} %all-to-all-done.1), kind=kLoop, calls=%fused_computation.4 | loop fusion | flops 917504 | bytes 5505024 | tf_op jit(solution)/shard_map/reduce_sum | solution.py:91
  183.7 0.0 copy-start.2
  183.7 0.0 copy-start.3
  183.7 2.9 %convolution_convert_fusion.1 = bf16[256,3584]{1,0:T(8,128)(2,1)} fusion(f32[256,256]{1,0:T(8,128)S(1)} %select_reduce_fusion, bf16[256,3584]{1,0:T(8,128)(2,1)S(1)} %bitcast.40), kind=kOutput, calls=%fused_computation.2 | convolution fusion | flops 2819489792 | bytes 3932160 | tf_op jit(solution)/shard_map/dot_general | solution.py:95
  186.6 0.0 reduce-scatter.2.cloned.1.call-update
  187.3 0.0 copy-done
  187.3 0.0 copy-done.2
  187.3 0.0 copy-done.3
  187.3 0.3 fusion.15
  187.7 0.2 fusion.36
  187.9 1.3 fusion.18
  189.2 54.5 %reduce-scatter.2.cloned.1.call-done = bf16[16,3584]{1,0:T(8,128)(2,1)} async-done(((bf16[256,3584]{1,0:T(8,128)(2,1)}), bf16[16,3584]{1,0:T(8,128)(2,1)}) %reduce-scatter.2.cloned.1.call-update) | async-done | bytes 114704 | tf_op jit(solution)/shard_map/reduce_scatter | solution.py:101
  (9 shorter events, 0.1 us)
Async XLA Ops:
  7.2 180.2 %copy-start = (bf16[4,64,576]{2,1,0:T(8,128)(2,1)S(1)}, bf16[4,64,576]{2,1,0:T(8,128)(2,1)}, u32[]{:S(2)}) copy-start(bf16[4,64,576]{2,1,0:T(8,128)(2,1)} %param.10) | copy-start | bytes 884740
  7.2 45.9 %all-gather.2.cloned.1.call-start = ((), (), s32[]{:S(2)}) async-start(), calls=%async_computation.3 | async-start | bytes 2019328 | tf_op jit(solution)/shard_map/all_gather | solution.py:52
  58.9 52.2 %copy-start.4 = (bf16[1,3584,512]{2,1,0:T(8,128)(2,1)S(1)}, bf16[1,3584,512]{2,1,0:T(8,128)(2,1)}, u32[]{:S(2)}) copy-start(bf16[1,3584,512]{2,1,0:T(8,128)(2,1)} %param.17) | copy-start | bytes 11010052
  109.3 1.8 copy-start.1
  123.2 57.6 %all-to-all-start.1 = ((bf16[16,32,3584]{2,1,0:T(8,128)(2,1)}), bf16[16,32,3584]{2,1,0:T(8,128)(2,1)}, u32[]{:S(2)}, u32[]{:S(2)}) async-start(bf16[16,32,3584]{2,1,0:T(8,128)(2,1)} %bitcast.41), calls=%async_computation.1 | async-start | bytes 7340032 | tf_op jit(solution)/shard_map/all_to_all | solution.py:81
  130.2 113.5 %reduce-scatter.2.cloned.1.call-start = ((), (), s32[]{:S(2)}) async-start(), calls=%async_computation.4 | async-start | bytes 1949696 | tf_op jit(solution)/shard_map/reduce_scatter | solution.py:101
  183.7 3.7 %copy-start.2 = (bf16[4,256,576]{1,2,0:T(8,128)(2,1)S(1)}, bf16[4,256,576]{1,2,0:T(8,128)(2,1)}, u32[]{:S(2)}) copy-start(bf16[4,256,576]{1,2,0:T(8,128)(2,1)} %param.11) | copy-start | bytes 3538948
  183.7 3.7 %copy-start.3 = (s32[4]{0:T(128)S(1)}, s32[4]{0:T(128)}, u32[]{:S(2)}) copy-start(s32[4]{0:T(128)} %param.12) | copy-start | bytes 52
Sparse Core Ops, SparseCore 0:
  10.6 42.4 all-gather.1
  186.8 56.8 reduce-scatter.1
where the time goes:
time: 251 us
  waiting for transfers between devices  146 us (58%)
  blocking collectives  50.4 us (20%)
  matrix products  18.8 us (7%)
  between operations  14.9 us (6%)
  other arithmetic  7.73 us (3%)
  starting transfers between devices  7.05 us (3%)
  local copies, waits for them, and re-layouts  5.71 us (2%)
    reduce_scatter x1, waiting for transfers between devices, per_device(): lax.psum_scatter(column_mixed.astype(jnp.bfloat16), 'grp', scatter_dimens...  54.5 us
    all_to_all x1, blocking collectives, per_device(): lax.all_to_all(doubled, 'ep', split_axis=0, concat_axis=0, tiled=True)  50.4 us
    all_to_all x1, waiting for transfers between devices, per_device(): lax.all_to_all(partials.reshape(peer_count, expert_slots, feature), 'ep',...  48.8 us
    all_gather x1, waiting for transfers between devices, per_device(): lax.all_gather(jnp.concatenate([tokens, meta], axis=1), 'grp', axis=0, ti...  42.6 us
    dot_general x1, matrix products, expert_partial(): return jnp.dot(hidden, w_down[0], preferred_element_type=jnp.float32)  10 us
    all_to_all x1, starting transfers between devices, per_device(): lax.all_to_all(partials.reshape(peer_count, expert_slots, feature), 'ep',...  6.97 us
  transfers between devices with their start and end apart: 3, of which 3 were waited for; matrix products, arithmetic and copies ran while one was open for 1% of the time, Pallas kernels for 0%

commit v1 on v0

--- a/solution.py
+++ b/solution.py
@@ -1,3 +1,4 @@
+import functools
 import jax
 import jax.numpy as jnp
 from jax import lax
@@ -8,6 +9,35 @@
 CAP = 2
 score_scale = 192.0 ** (-0.5)
 neg_large = -1e30
+
+
+def slabs_balance(v0, axis_k):
+    runs = []
+    workers = lax.axis_size("grp")
+    b = 0
+    while b < workers:
+        runs.append((b, (b + 1) % workers))
+        b += 1
+    in_order = []
+    b = 0
+    while b < workers:
+        in_order.append((b, (b - 1) % workers))
+        b += 1
+    response, later = ([v0], [v0])
+    for _ in range(workers // 2):
+        response.append(lax.ppermute(response[-1], axis_name="grp", perm=runs))
+    rr = 0
+    while rr < (workers - 1) // 2:
+        later.append(lax.ppermute(later[-1], perm=in_order, axis_name="grp"))
+        rr += 1
+    small = jnp.concatenate([*response[::-1], *later[1:]], axis=axis_k)
+    g_now = jnp.roll(
+        small, shift=(lax.axis_index("grp") - workers // 2) * v0.shape[axis_k], axis=axis_k
+    )
+    return g_now
+
+
+write_layers_all_for = functools.partial(slabs_balance, axis_k=0)
 
 
 def attend(queries, cache, lengths, live_count):
@@ -49,7 +79,7 @@
     gate_low = (gates - gate_high.astype(jnp.float32)).astype(jnp.bfloat16)
     meta = jnp.concatenate([ids.astype(jnp.bfloat16), gate_high, gate_low], axis=1)
     meta = jnp.pad(meta, ((0, 0), (0, 128 - meta.shape[1])))
-    packed = lax.all_gather(jnp.concatenate([tokens, meta], axis=1), "grp", axis=0, tiled=True)
+    packed = write_layers_all_for(jnp.concatenate([tokens, meta], axis=1))
     all_tokens = packed[:, :feature]
     all_ids = packed[:, feature : feature + TOPK].astype(jnp.int32)
     all_gates = packed[:, feature + TOPK : feature + 2 * TOPK].astype(jnp.float32) + packed[

time: 251 us -> 312 us (1.24); the launches traced: 251 us -> 308 us
  local copies, waits for them, and re-layouts: 5.71 us -> 60.8 us
  starting transfers between devices: 7.05 us -> 31.1 us
  waiting for transfers between devices: 146 us -> 127 us
  blocking collectives: 50.4 us -> 46.5 us
    all_gather x1 -> x0, waiting for transfers between devices: 42.6 us -> none  [per_device(): lax.all_gather(jnp.concatenate([tokens, meta], axis=1), 'grp', axis=0, ti...]
    concatenate x0 -> x2, local copies, waits for them, and re-layouts: none -> 31 us  [the longest x1 30.5 us: slabs_balance(): jnp.roll(small, shift=(lax.axis_index('grp') - workers // 2) * v0.shape[a...]
    ppermute x0 -> x15, local copies, waits for them, and re-layouts: none -> 25.3 us  [the longest x8 13.3 us: slabs_balance(): response.append(lax.ppermute(response[-1], axis_name='grp', perm=runs))]
    ppermute x0 -> x15, starting transfers between devices: none -> 23.2 us  [the longest x7 23.2 us: slabs_balance(): later.append(lax.ppermute(later[-1], perm=in_order, axis_name='grp'))]
    reduce_scatter x1, waiting for transfers between devices: 54.5 us -> 72.1 us  [per_device(): lax.psum_scatter(column_mixed.astype(jnp.bfloat16), 'grp', scatter_dimens...]
    ppermute x0 -> x15, waiting for transfers between devices: none -> 17.5 us  [the longest x8 17.5 us: slabs_balance(): response.append(lax.ppermute(response[-1], axis_name='grp', perm=runs))]
    all_to_all x1, waiting for transfers between devices: 48.8 us -> 36.9 us  [per_device(): lax.all_to_all(partials.reshape(peer_count, expert_slots, feature), 'ep',...]
    all_to_all x1, blocking collectives: 50.4 us -> 46.5 us  [per_device(): lax.all_to_all(doubled, 'ep', split_axis=0, concat_axis=0, tiled=True)]
  transfers between devices with their start and end apart: 3 -> 17, of which waited for: 3 -> 9; matrix products, arithmetic and copies ran while one was open for 1% -> 9% of each run, Pallas kernels for 0% -> 0%
where the time goes in v1:
time: 312 us; the launch traced here: 308 us
  waiting for transfers between devices  127 us (41%)
  local copies, waits for them, and re-layouts  60.8 us (19%)
  blocking collectives  46.5 us (15%)
  starting transfers between devices  31.1 us (10%)
  matrix products  19.7 us (6%)
  between operations  15 us (5%)
  other arithmetic  8.61 us (3%)
    reduce_scatter x1, waiting for transfers between devices, per_device(): lax.psum_scatter(column_mixed.astype(jnp.bfloat16), 'grp', scatter_dimens...  72.1 us
    all_to_all x1, blocking collectives, per_device(): lax.all_to_all(doubled, 'ep', split_axis=0, concat_axis=0, tiled=True)  46.5 us
    all_to_all x1, waiting for transfers between devices, per_device(): lax.all_to_all(partials.reshape(peer_count, expert_slots, feature), 'ep',...  36.9 us
    concatenate x1, local copies, waits for them, and re-layouts, slabs_balance(): jnp.roll(small, shift=(lax.axis_index('grp') - workers // 2) * v0.shape[a...  30.5 us
    ppermute x7, starting transfers between devices, slabs_balance(): later.append(lax.ppermute(later[-1], perm=in_order, axis_name='grp'))  23.2 us
    ppermute x8, waiting for transfers between devices, slabs_balance(): response.append(lax.ppermute(response[-1], axis_name='grp', perm=runs))  17.5 us
    ppermute x8, local copies, waits for them, and re-layouts, slabs_balance(): response.append(lax.ppermute(response[-1], axis_name='grp', perm=runs))  13.3 us
    ppermute x7, local copies, waits for them, and re-layouts, slabs_balance(): later.append(lax.ppermute(later[-1], perm=in_order, axis_name='grp'))  11.9 us
  transfers between devices with their start and end apart: 17, of which 9 were waited for; matrix products, arithmetic and copies ran while one was open for 9% of the time, Pallas kernels for 0%

profile of v1, /device:TPU:6, one launch (start us, length us, event | category | flops | bytes accessed | tf_op | source)
XLA Modules:
  0.0 308.2 jit_solution(10292522962695799508)
XLA Ops:
  7.2 0.8 copy.35
  8.0 0.8 copy.34
  8.8 0.1 fusion.31
  8.8 0.9 pad_maximum_fusion
  9.7 0.0 collective-permute-start
  9.8 5.3 %collective-permute-start.8 = (bf16[16,3712]{1,0:T(8,128)(2,1)S(1)}, bf16[16,3712]{1,0:T(8,128)(2,1)S(1)}, u32[]{:S(2)}, u32[]{:S(2)}) collective-permute-start(bf16[16,3712]{1,0:T(8,128)(2,1)S(1)} %pad_maximum_fusion), channel_id=1, source_target_pairs={{0,240},{16,0},{32,16},{48,32},{64,48},{80,64},{96,80},{112,96},{1... | collective-permute-start | bytes 356360 | tf_op jit(solution)/shard_map/ppermute | solution.py:31
  15.1 2.5 collective-permute-done
  17.6 3.0 collective-permute-start.9
  20.5 2.5 collective-permute-done.1
  23.0 3.0 collective-permute-start.10
  26.0 2.5 collective-permute-done.2
  28.5 3.0 collective-permute-start.11
  31.5 2.5 collective-permute-done.3
  34.0 3.0 collective-permute-start.12
  37.0 2.5 collective-permute-done.4
  39.5 3.0 collective-permute-start.13
  42.4 2.5 collective-permute-done.5
  45.0 3.1 collective-permute-start.14
  48.0 2.5 collective-permute-done.6
  50.5 0.5 copy.45
  51.1 0.5 copy.44
  51.6 0.5 copy.46
  52.1 1.4 copy.43
  53.4 1.3 copy.47
  54.7 2.2 copy.42
  57.0 2.2 copy.48
  59.2 1.4 copy.41
  60.5 1.4 copy.49
  61.9 1.3 copy.40
  63.2 2.2 copy.50
  65.4 2.2 copy.39
  67.6 2.2 copy.51
  69.8 2.2 copy.38
  72.0 2.2 copy.52
  74.2 2.2 copy.37
  76.4 30.5 %concatenate.14 = bf16[512,3712]{0,1:T(8,128)(2,1)} concatenate(bf16[16,3712]{0,1:T(8,128)(2,1)} %copy.37, bf16[16,3712]{0,1:T(8,128)(2,1)} %copy.38, bf16[16,3712]{0,1:T(8,128)(2,1)} %copy.39, bf16[16,3712]{0,1:T(8,128)(2,1)} %copy.40, bf16[16,3712]{0,1:T(8,128)(2,1)} %copy.41, bf16[16,3712]{0,1:T(8,128)(2,1)} %copy.42, bf16[16,3712]{0,1:T(8,128)(2,1)} %copy.43, ...), dimensions={0} | concatenate | bytes 7602176 | tf_op jit(solution)/shard_map/jit(_roll_dynamic)/concatenate | solution.py:34
  106.9 0.8 convert_subtract_fusion
  107.7 0.1 reshape.114
  107.8 0.1 copy.69
  107.9 0.7 fusion.38
  108.6 0.1 copy.70
  108.7 0.1 reduce_window_sum.14
  108.8 0.1 add_select_fusion
  108.9 0.1 copy.71
  109.0 0.7 fusion.6
  109.7 3.0 convolution_convert_fusion.1
  112.8 0.4 broadcast_in_dim.46
  113.2 46.5 %all_to_all.10 = bf16[16,32,3584]{2,1,0:T(8,128)(2,1)S(1)} all-to-all(bf16[16,32,3584]{2,1,0:T(8,128)(2,1)S(1)} %bitcast.37), channel_id=1, replica_groups=mesh['grp'=16,'ep'=16] {'ep'}, dimensions={0} | all-to-all | bytes 7340032 | tf_op jit(solution)/shard_map/all_to_all | solution.py:107
  159.7 1.9 copy-done.1
  161.6 2.0 fusion.4
  163.6 10.1 %convolution_convert_fusion = bf16[512,3584]{1,0:T(8,128)(2,1)} fusion(bf16[1,512,3584]{2,1,0:T(8,128)(2,1)} %param.19, bf16[512,3584]{1,0:T(8,128)(2,1)} %bitcast.42, bf16[1,3584,512]{2,1,0:T(8,128)(2,1)} %param.18, f32[512,512]{1,0:T(8,128)S(1)} %fusion.4), kind=kOutput, calls=%fused_computation.1 | convolution fusion | flops 3761504256 | bytes 15728640 | tf_op jit(solution)/shard_map/dot_general | solution.py:65
  173.7 7.6 %all-to-all-start.1 = ((bf16[16,32,3584]{2,1,0:T(8,128)(2,1)}), bf16[16,32,3584]{2,1,0:T(8,128)(2,1)}, u32[]{:S(2)}, u32[]{:S(2)}) async-start(bf16[16,32,3584]{2,1,0:T(8,128)(2,1)} %bitcast.40), calls=%async_computation.1 | async-start | bytes 7340032 | tf_op jit(solution)/shard_map/all_to_all | solution.py:111
  181.3 0.2 reduce-scatter.2.cloned.1.call-start
  181.6 0.8 convert_add_fusion
  182.4 0.1 copy.72
  182.5 1.5 select_reduce_fusion
  184.0 36.9 %all-to-all-done.1 = bf16[16,32,3584]{2,1,0:T(8,128)(2,1)} async-done(((bf16[16,32,3584]{2,1,0:T(8,128)(2,1)}), bf16[16,32,3584]{2,1,0:T(8,128)(2,1)}, u32[]{:S(2)}, u32[]{:S(2)}) %all-to-all-start.1) | async-done | bytes 3670048 | tf_op jit(solution)/shard_map/all_to_all | solution.py:111
  220.9 2.8 bitcast_reduce_fusion
  223.8 2.9 convolution_convert_fusion.2
  226.7 0.0 reduce-scatter.2.cloned.1.call-update
  227.4 0.3 fusion.15
  227.8 0.2 fusion.37
  228.0 1.3 fusion.18
  229.3 72.1 %reduce-scatter.2.cloned.1.call-done = bf16[16,3584]{1,0:T(8,128)(2,1)} async-done(((bf16[256,3584]{1,0:T(8,128)(2,1)}), bf16[16,3584]{1,0:T(8,128)(2,1)}) %reduce-scatter.2.cloned.1.call-update) | async-done | bytes 114704 | tf_op jit(solution)/shard_map/reduce_scatter | solution.py:131
  (51 shorter events, 0.2 us)
Async XLA Ops:
  7.2 220.2 %copy-start = (bf16[4,64,576]{2,1,0:T(8,128)(2,1)S(1)}, bf16[4,64,576]{2,1,0:T(8,128)(2,1)}, u32[]{:S(2)}) copy-start(bf16[4,64,576]{2,1,0:T(8,128)(2,1)} %param.10) | copy-start | bytes 884740
  9.7 7.8 %collective-permute-start = (bf16[16,3712]{1,0:T(8,128)(2,1)S(1)}, bf16[16,3712]{1,0:T(8,128)(2,1)S(1)}, u32[]{:S(2)}, u32[]{:S(2)}) collective-permute-start(bf16[16,3712]{1,0:T(8,128)(2,1)S(1)} %pad_maximum_fusion), channel_id=1, source_target_pairs={{0,16},{16,32},{32,48},{48,64},{64,80},{80,96},{96,112},{112,128},... | collective-permute-start | bytes 356360 | tf_op jit(solution)/shard_map/ppermute | solution.py:28
  9.8 7.8 %collective-permute-start.8 = (bf16[16,3712]{1,0:T(8,128)(2,1)S(1)}, bf16[16,3712]{1,0:T(8,128)(2,1)S(1)}, u32[]{:S(2)}, u32[]{:S(2)}) collective-permute-start(bf16[16,3712]{1,0:T(8,128)(2,1)S(1)} %pad_maximum_fusion), channel_id=1, source_target_pairs={{0,240},{16,0},{32,16},{48,32},{64,48},{80,64},{96,80},{112,96},{1... | collective-permute-start | bytes 356360 | tf_op jit(solution)/shard_map/ppermute | solution.py:31
  17.6 5.5 %collective-permute-start.1 = (bf16[16,3712]{1,0:T(8,128)(2,1)S(1)}, bf16[16,3712]{1,0:T(8,128)(2,1)S(1)}, u32[]{:S(2)}, u32[]{:S(2)}) collective-permute-start(bf16[16,3712]{1,0:T(8,128)(2,1)S(1)} %collective-permute-done), channel_id=1, source_target_pairs={{0,16},{16,32},{32,48},{48,64},{64,80},{80,96},{96,112},{112,128},... | collective-permute-start | bytes 356360 | tf_op jit(solution)/shard_map/ppermute | solution.py:28
  17.6 5.5 %collective-permute-start.9 = (bf16[16,3712]{1,0:T(8,128)(2,1)S(1)}, bf16[16,3712]{1,0:T(8,128)(2,1)S(1)}, u32[]{:S(2)}, u32[]{:S(2)}) collective-permute-start(bf16[16,3712]{1,0:T(8,128)(2,1)S(1)} %collective-permute-done.8), channel_id=1, source_target_pairs={{0,240},{16,0},{32,16},{48,32},{64,48},{80,64},{96,80},{112,96},{1... | collective-permute-start | bytes 356360 | tf_op jit(solution)/shard_map/ppermute | solution.py:31
  23.0 5.5 %collective-permute-start.2 = (bf16[16,3712]{1,0:T(8,128)(2,1)S(1)}, bf16[16,3712]{1,0:T(8,128)(2,1)S(1)}, u32[]{:S(2)}, u32[]{:S(2)}) collective-permute-start(bf16[16,3712]{1,0:T(8,128)(2,1)S(1)} %collective-permute-done.1), channel_id=1, source_target_pairs={{0,16},{16,32},{32,48},{48,64},{64,80},{80,96},{96,112},{112,128},... | collective-permute-start | bytes 356360 | tf_op jit(solution)/shard_map/ppermute | solution.py:28
  23.0 5.5 %collective-permute-start.10 = (bf16[16,3712]{1,0:T(8,128)(2,1)S(1)}, bf16[16,3712]{1,0:T(8,128)(2,1)S(1)}, u32[]{:S(2)}, u32[]{:S(2)}) collective-permute-start(bf16[16,3712]{1,0:T(8,128)(2,1)S(1)} %collective-permute-done.9), channel_id=1, source_target_pairs={{0,240},{16,0},{32,16},{48,32},{64,48},{80,64},{96,80},{112,96},{1... | collective-permute-start | bytes 356360 | tf_op jit(solution)/shard_map/ppermute | solution.py:31
  28.5 22.5 %copy-start.3 = (bf16[16,3712]{1,0:T(8,128)(2,1)}, bf16[16,3712]{1,0:T(8,128)(2,1)S(1)}, u32[]{:S(2)}) copy-start(bf16[16,3712]{1,0:T(8,128)(2,1)S(1)} %collective-permute-done.2) | copy-start | bytes 356356
  28.5 5.5 %collective-permute-start.3 = (bf16[16,3712]{1,0:T(8,128)(2,1)S(1)}, bf16[16,3712]{1,0:T(8,128)(2,1)S(1)}, u32[]{:S(2)}, u32[]{:S(2)}) collective-permute-start(bf16[16,3712]{1,0:T(8,128)(2,1)S(1)} %collective-permute-done.2), channel_id=1, source_target_pairs={{0,16},{16,32},{32,48},{48,64},{64,80},{80,96},{96,112},{112,128},... | collective-permute-start | bytes 356360 | tf_op jit(solution)/shard_map/ppermute | solution.py:28
  28.5 22.5 %copy-start.4 = (bf16[16,3712]{1,0:T(8,128)(2,1)}, bf16[16,3712]{1,0:T(8,128)(2,1)S(1)}, u32[]{:S(2)}) copy-start(bf16[16,3712]{1,0:T(8,128)(2,1)S(1)} %collective-permute-done.10) | copy-start | bytes 356356
  28.5 5.5 %collective-permute-start.11 = (bf16[16,3712]{1,0:T(8,128)(2,1)S(1)}, bf16[16,3712]{1,0:T(8,128)(2,1)S(1)}, u32[]{:S(2)}, u32[]{:S(2)}) collective-permute-start(bf16[16,3712]{1,0:T(8,128)(2,1)S(1)} %collective-permute-done.10), channel_id=1, source_target_pairs={{0,240},{16,0},{32,16},{48,32},{64,48},{80,64},{96,80},{112,96},{1... | collective-permute-start | bytes 356360 | tf_op jit(solution)/shard_map/ppermute | solution.py:31
  34.0 17.1 %copy-start.5 = (bf16[16,3712]{1,0:T(8,128)(2,1)}, bf16[16,3712]{1,0:T(8,128)(2,1)S(1)}, u32[]{:S(2)}) copy-start(bf16[16,3712]{1,0:T(8,128)(2,1)S(1)} %collective-permute-done.3) | copy-start | bytes 356356
  34.0 5.5 %collective-permute-start.4 = (bf16[16,3712]{1,0:T(8,128)(2,1)S(1)}, bf16[16,3712]{1,0:T(8,128)(2,1)S(1)}, u32[]{:S(2)}, u32[]{:S(2)}) collective-permute-start(bf16[16,3712]{1,0:T(8,128)(2,1)S(1)} %collective-permute-done.3), channel_id=1, source_target_pairs={{0,16},{16,32},{32,48},{48,64},{64,80},{80,96},{96,112},{112,128},... | collective-permute-start | bytes 356360 | tf_op jit(solution)/shard_map/ppermute | solution.py:28
  34.0 17.0 %copy-start.7 = (bf16[16,3712]{1,0:T(8,128)(2,1)}, bf16[16,3712]{1,0:T(8,128)(2,1)S(1)}, u32[]{:S(2)}) copy-start(bf16[16,3712]{1,0:T(8,128)(2,1)S(1)} %collective-permute-done.11) | copy-start | bytes 356356
  34.0 5.5 %collective-permute-start.12 = (bf16[16,3712]{1,0:T(8,128)(2,1)S(1)}, bf16[16,3712]{1,0:T(8,128)(2,1)S(1)}, u32[]{:S(2)}, u32[]{:S(2)}) collective-permute-start(bf16[16,3712]{1,0:T(8,128)(2,1)S(1)} %collective-permute-done.11), channel_id=1, source_target_pairs={{0,240},{16,0},{32,16},{48,32},{64,48},{80,64},{96,80},{112,96},{1... | collective-permute-start | bytes 356360 | tf_op jit(solution)/shard_map/ppermute | solution.py:31
  39.5 11.6 %copy-start.9 = (bf16[16,3712]{1,0:T(8,128)(2,1)}, bf16[16,3712]{1,0:T(8,128)(2,1)S(1)}, u32[]{:S(2)}) copy-start(bf16[16,3712]{1,0:T(8,128)(2,1)S(1)} %collective-permute-done.4) | copy-start | bytes 356356
  39.5 5.5 %collective-permute-start.5 = (bf16[16,3712]{1,0:T(8,128)(2,1)S(1)}, bf16[16,3712]{1,0:T(8,128)(2,1)S(1)}, u32[]{:S(2)}, u32[]{:S(2)}) collective-permute-start(bf16[16,3712]{1,0:T(8,128)(2,1)S(1)} %collective-permute-done.4), channel_id=1, source_target_pairs={{0,16},{16,32},{32,48},{48,64},{64,80},{80,96},{96,112},{112,128},... | collective-permute-start | bytes 356360 | tf_op jit(solution)/shard_map/ppermute | solution.py:28
  39.5 11.6 %copy-start.11 = (bf16[16,3712]{1,0:T(8,128)(2,1)}, bf16[16,3712]{1,0:T(8,128)(2,1)S(1)}, u32[]{:S(2)}) copy-start(bf16[16,3712]{1,0:T(8,128)(2,1)S(1)} %collective-permute-done.12) | copy-start | bytes 356356
  39.5 5.5 %collective-permute-start.13 = (bf16[16,3712]{1,0:T(8,128)(2,1)S(1)}, bf16[16,3712]{1,0:T(8,128)(2,1)}, u32[]{:S(2)}, u32[]{:S(2)}) collective-permute-start(bf16[16,3712]{1,0:T(8,128)(2,1)S(1)} %collective-permute-done.12), channel_id=1, source_target_pairs={{0,240},{16,0},{32,16},{48,32},{64,48},{80,64},{96,80},{112,96},{1... | collective-permute-start | bytes 356360 | tf_op jit(solution)/shard_map/ppermute | solution.py:31
  44.9 6.1 %copy-start.12 = (bf16[16,3712]{1,0:T(8,128)(2,1)}, bf16[16,3712]{1,0:T(8,128)(2,1)S(1)}, u32[]{:S(2)}) copy-start(bf16[16,3712]{1,0:T(8,128)(2,1)S(1)} %collective-permute-done.5) | copy-start | bytes 356356
  44.9 5.6 %collective-permute-start.6 = (bf16[16,3712]{1,0:T(8,128)(2,1)S(1)}, bf16[16,3712]{1,0:T(8,128)(2,1)}, u32[]{:S(2)}, u32[]{:S(2)}) collective-permute-start(bf16[16,3712]{1,0:T(8,128)(2,1)S(1)} %collective-permute-done.5), channel_id=1, source_target_pairs={{0,16},{16,32},{32,48},{48,64},{64,80},{80,96},{96,112},{112,128},... | collective-permute-start | bytes 356360 | tf_op jit(solution)/shard_map/ppermute | solution.py:28
  45.0 27.0 %collective-permute-start.14 = (bf16[16,3712]{1,0:T(8,128)(2,1)}, bf16[16,3712]{1,0:T(8,128)(2,1)}, u32[]{:S(2)}, u32[]{:S(2)}) collective-permute-start(bf16[16,3712]{1,0:T(8,128)(2,1)} %collective-permute-done.13), channel_id=1, source_target_pairs={{0,240},{16,0},{32,16},{48,32},{64,48},{80,64},{96,80},{112,96},{1... | collective-permute-start | bytes 356360 | tf_op jit(solution)/shard_map/ppermute | solution.py:31
  50.5 23.7 %collective-permute-start.7 = (bf16[16,3712]{1,0:T(8,128)(2,1)}, bf16[16,3712]{1,0:T(8,128)(2,1)}, u32[]{:S(2)}, u32[]{:S(2)}) collective-permute-start(bf16[16,3712]{1,0:T(8,128)(2,1)} %collective-permute-done.6), channel_id=1, source_target_pairs={{0,16},{16,32},{32,48},{48,64},{64,80},{80,96},{96,112},{112,128},... | collective-permute-start | bytes 356360 | tf_op jit(solution)/shard_map/ppermute | solution.py:28
  52.1 7.1 %copy-start.6 = (bf16[16,3712]{1,0:T(8,128)(2,1)S(1)}, bf16[16,3712]{1,0:T(8,128)(2,1)}, u32[]{:S(2)}) copy-start(bf16[16,3712]{1,0:T(8,128)(2,1)} %copy-done.5) | copy-start | bytes 356356
  53.4 7.1 %copy-start.8 = (bf16[16,3712]{1,0:T(8,128)(2,1)S(1)}, bf16[16,3712]{1,0:T(8,128)(2,1)}, u32[]{:S(2)}) copy-start(bf16[16,3712]{1,0:T(8,128)(2,1)} %copy-done.7) | copy-start | bytes 356356
  54.7 7.2 %copy-start.10 = (bf16[16,3712]{1,0:T(8,128)(2,1)S(1)}, bf16[16,3712]{1,0:T(8,128)(2,1)}, u32[]{:S(2)}) copy-start(bf16[16,3712]{1,0:T(8,128)(2,1)} %copy-done.9) | copy-start | bytes 356356
  113.1 48.4 %copy-start.14 = (bf16[1,3584,512]{2,1,0:T(8,128)(2,1)S(1)}, bf16[1,3584,512]{2,1,0:T(8,128)(2,1)}, u32[]{:S(2)}) copy-start(bf16[1,3584,512]{2,1,0:T(8,128)(2,1)} %param.17) | copy-start | bytes 11010052
  159.7 1.9 copy-start.1
  173.7 47.2 %all-to-all-start.1 = ((bf16[16,32,3584]{2,1,0:T(8,128)(2,1)}), bf16[16,32,3584]{2,1,0:T(8,128)(2,1)}, u32[]{:S(2)}, u32[]{:S(2)}) async-start(bf16[16,32,3584]{2,1,0:T(8,128)(2,1)} %bitcast.40), calls=%async_computation.1 | async-start | bytes 7340032 | tf_op jit(solution)/shard_map/all_to_all | solution.py:111
  181.3 120.0 %reduce-scatter.2.cloned.1.call-start = ((), (), s32[]{:S(2)}) async-start(), calls=%async_computation.3 | async-start | bytes 1949696 | tf_op jit(solution)/shard_map/reduce_scatter | solution.py:131
  223.7 3.6 %copy-start.2 = (bf16[4,256,576]{1,2,0:T(8,128)(2,1)S(1)}, bf16[4,256,576]{1,2,0:T(8,128)(2,1)}, u32[]{:S(2)}) copy-start(bf16[4,256,576]{1,2,0:T(8,128)(2,1)} %param.11) | copy-start | bytes 3538948
  223.8 3.6 %copy-start.13 = (s32[4]{0:T(128)S(1)}, s32[4]{0:T(128)}, u32[]{:S(2)}) copy-start(s32[4]{0:T(128)} %param.12) | copy-start | bytes 52
Sparse Core Ops, SparseCore 0:
  226.8 74.4 reduce-scatter.1
